TPU v7x, 32 devices: a whole 2x2x4 slice. The times are simulated.
32 devices in a mesh: narrow: 4 (over y, core), wide: 8 (over z, x).
Axes of the slice: x: 2, y: 2, z: 4, core: 2. Of those that a mesh axis runs over, the one named last changes fastest.
Arguments:
- normed: bfloat16 [1024, 2048], P('wide', 'narrow'), may hold values from -6 to 6
- router_weight: bfloat16 [2048, 128], P('narrow'), may hold values from -0.125 to 0.125
- gate_up_weight: bfloat16 [128, 2, 2048, 768], P('wide', None, 'narrow'), may hold values from -0.1875 to 0.1875
- down_weight: bfloat16 [128, 768, 2048], P('wide', 'narrow'), may hold values from -0.3125 to 0.3125
- expert_ids: int32 [1024, 8], P('wide'), may hold values from 0 to 127, all different within a row; in each aligned block of 128 rows (0 to 127, 128 to 255, ...) at most 16 rows name the same one
Outputs:
- mixed: bfloat16 [1024, 2048], P('wide', 'narrow')
Inputs may be any that keep to these rules, and one draw needn't show every extreme that they name: `expert_ids`: each row names 8 different experts. In each aligned block of 128 rows (the rows of one index of wide) no expert is named by more than 16 rows, and in every draw some expert is named by exactly 16 rows of some block.
All inputs are finite; a program needn't handle non-finite values.
Results may differ from a plain program's by a relative error of at most 0.023.
Values may be sent and summed in bfloat16 or wider, within the bound.
No kernel may reach another device: no remote copies, remote signals or barrier semaphores. Data moves between devices by JAX's collectives and lax.ppermute only.
A program may use at most 128 MiB of HBM per device.

v0:
```python
import jax
import jax.numpy as jnp
from jax import lax
from jax.sharding import PartitionSpec as P

TOPK = 8
CAP = 16


def local(normed, router_weight, gate_up_weight, down_weight, expert_ids):
    tok_count = normed.shape[0]
    share_width = normed.shape[1]
    experts = router_weight.shape[1]
    local_experts = gate_up_weight.shape[0]
    capacity = CAP
    blocks = lax.axis_size("wide")
    pair_count = tok_count * TOPK
    logits = lax.psum(
        jnp.dot(normed, router_weight, preferred_element_type=jnp.float32).astype(jnp.bfloat16),
        "narrow",
    ).astype(jnp.float32)
    picker = (expert_ids[:, :, None] == jnp.arange(experts, dtype=jnp.int32)[None, None, :]).astype(
        jnp.float32
    )
    chosen = jnp.sum(picker * logits[:, None, :], axis=2)
    scores = jnp.exp(chosen)
    weights = scores / jnp.sum(scores, axis=1, keepdims=True)
    pair_ids = expert_ids.reshape(-1)
    onehot = (pair_ids[:, None] == jnp.arange(experts, dtype=jnp.int32)[None, :]).astype(jnp.int32)
    running = jnp.cumsum(onehot, axis=0) - onehot
    order_in = jnp.sum(running * onehot, axis=1)
    owner = pair_ids // local_experts
    local_of_pair = pair_ids - owner * local_experts
    out_index = (local_of_pair * blocks + owner) * capacity + order_in
    token_in_block = jnp.arange(pair_count, dtype=jnp.int32) // TOPK
    slot_total = local_experts * blocks * capacity
    gathered, all_ids = (
        lax.all_gather(normed, "wide", axis=0, tiled=True),
        lax.all_gather(expert_ids.astype(jnp.bfloat16), "wide", axis=0, tiled=True),
    )
    all_ids = all_ids.astype(jnp.int32).reshape(blocks, pair_count)
    first_expert = lax.axis_index("wide") * local_experts
    local_ids = all_ids - first_expert
    local_hot = (
        local_ids[:, :, None] == jnp.arange(local_experts, dtype=jnp.int32)[None, None, :]
    ).astype(jnp.int32)
    local_running = jnp.cumsum(local_hot, axis=1) - local_hot
    order_all = jnp.sum(local_running * local_hot, axis=2)
    block_index = jnp.arange(blocks, dtype=jnp.int32)[:, None]
    is_mine = (local_ids >= 0) & (local_ids < local_experts)
    destination = jnp.where(
        is_mine, (local_ids * blocks + block_index) * capacity + order_all, slot_total
    )
    source_token = block_index * tok_count + token_in_block[None, :]
    slot_table = (
        jnp.full((slot_total,), blocks * tok_count, jnp.int32)
        .at[destination.reshape(-1)]
        .set(source_token.reshape(-1), mode="drop")
    )
    padded = jnp.concatenate([gathered, jnp.zeros((1, share_width), gathered.dtype)], axis=0)
    arrived = padded[slot_table].reshape(local_experts, blocks, capacity, share_width)
    slot_rows = arrived.reshape(local_experts, blocks * capacity, share_width)
    gate_terms = jnp.einsum(
        "erd,edf->erf", slot_rows, gate_up_weight[:, 0], preferred_element_type=jnp.float32
    )
    up_terms = jnp.einsum(
        "erd,edf->erf", slot_rows, gate_up_weight[:, 1], preferred_element_type=jnp.float32
    )
    gate_sum, up_sum = (
        lax.psum_scatter(
            gate_terms.astype(jnp.bfloat16), "narrow", scatter_dimension=2, tiled=True
        ).astype(jnp.float32),
        lax.psum_scatter(
            up_terms.astype(jnp.bfloat16), "narrow", scatter_dimension=2, tiled=True
        ).astype(jnp.float32),
    )
    hidden = (jax.nn.silu(gate_sum) * up_sum).astype(jnp.bfloat16)
    expert_terms = jnp.einsum(
        "erf,efd->erd", hidden, down_weight, preferred_element_type=jnp.float32
    )
    expert_out = lax.psum_scatter(
        expert_terms.astype(jnp.bfloat16), "narrow", scatter_dimension=2, tiled=True
    )
    expert_out = expert_out.reshape(local_experts, blocks, capacity, share_width)
    returned = lax.all_to_all(expert_out, "wide", split_axis=1, concat_axis=1, tiled=True)
    flat_out = returned.reshape(slot_total, share_width)
    picked = flat_out[out_index].reshape(tok_count, TOPK, share_width)
    combined = jnp.sum(weights[:, :, None] * picked.astype(jnp.float32), axis=1)
    return combined.astype(jnp.bfloat16)


def solution(mesh):
    placed = (
        P("wide", "narrow"),
        P("narrow", None),
        P("wide", None, "narrow", None),
        P("wide", "narrow", None),
        P("wide", None),
    )
    return jax.shard_map(
        local, mesh=mesh, in_specs=placed, out_specs=P("wide", "narrow"), check_vma=False
    )
```

profile of v0, /device:TPU:0, one launch (start us, length us, event | category | flops | bytes accessed | tf_op | source)
XLA Modules:
  0.0 355.1 jit_solution(15422865398020943970)
XLA Ops:
  6.5 0.7 all-gather.2.cloned.1.call-update
  7.3 0.7 convert_element_type.56
  8.0 27.9 %all_gather.7 = bf16[1024,8]{0,1:T(8,128)(2,1)S(1)} all-gather(bf16[128,8]{0,1:T(8,128)(2,1)S(1)} %convert_element_type.56), channel_id=1, replica_groups=mesh['narrow'=4,'wide'=8] {'wide'}, dimensions={0}, use_global_device_ids=true | all-gather | bytes 18432 | tf_op jit(solution)/shard_map/all_gather | solution.py:39
  36.2 0.3 sub.55
  36.4 0.3 sub.54
  36.8 36.0 %reduce-window.14 = s32[8,16,8,128]{3,2,1,0:T(8,128)S(1)} reduce-window(s32[8,16,8,128]{3,2,1,0:T(8,128)S(1)} %fusion.26, s32[]{:T(128)} %constant.58.clone.1), window={size=1x1x1x128 pad=0_0x0_0x0_0x127_0}, to_apply=%region_3.0 | reduce-window | flops 16646144 | bytes 1048580 | tf_op jit(solution)/shard_map/reduce-window
  72.8 0.2 slice.28
  73.0 0.5 copy.42
  73.6 0.2 broadcast_add_fusion.1
  74.3 0.3 mul.105
  74.6 0.3 copy.38
  74.9 0.3 and.47
  75.4 30.4 %scatter_custom_fusion = s32[2048]{0:T(1024)S(1)} fusion(s32[8192]{0:T(1024)S(1)} %bitcast.67, s32[8192]{0:T(1024)S(1)} %bitcast.68, s32[]{:T(128)} %constant.55.clone.1), kind=kCustom, calls=%fused_computation.64 | custom fusion | bytes 8196 | tf_op jit(solution)/shard_map/scatter | solution.py:58
  105.9 1.3 concatenate.3
  107.2 7.5 %gather_fusion = bf16[2048,512]{1,0:T(8,128)(2,1)S(1)} fusion(bf16[1025,512]{1,0:T(8,128)(2,1)S(1)} %concatenate.3, s32[2048]{0:T(1024)S(1)} %fusion.28), kind=kCustom, calls=%fused_computation | custom fusion | bytes 4202496 | tf_op jit(solution)/shard_map/gather | solution.py:61
  114.7 9.9 %fusion.6 = bf16[16,128,768]{1,2,0:T(8,128)(2,1)} fusion(bf16[16,128,512]{2,1,0:T(8,128)(2,1)S(1)} %bitcast.60, bf16[16,2,512,768]{3,2,1,0:T(8,128)(2,1)} %param.7), kind=kOutput, calls=%fused_computation.10 | convolution fusion | flops 1612185600 | bytes 17825792 | tf_op jit(solution)/shard_map/erd,edf->erf/dot_general | solution.py:63
  124.7 0.2 reduce-scatter.6.cloned.1.call-start
  124.9 10.0 %fusion.9 = bf16[16,128,768]{1,2,0:T(8,128)(2,1)} fusion(bf16[16,128,512]{2,1,0:T(8,128)(2,1)S(1)} %bitcast.61, bf16[16,2,512,768]{3,2,1,0:T(8,128)(2,1)} %param.7), kind=kOutput, calls=%fused_computation.11 | convolution fusion | flops 1612185600 | bytes 17825792 | tf_op jit(solution)/shard_map/erd,edf->erf/dot_general | solution.py:66
  134.9 27.1 %reduce-scatter.4.cloned.1.call-done = bf16[16,128,192]{1,2,0:T(8,128)(2,1)} async-done(((bf16[16,128,768]{1,2,0:T(8,128)(2,1)}), bf16[16,128,192]{1,2,0:T(8,128)(2,1)}) %reduce-scatter.4.cloned.1.call-update) | async-done | bytes 786448 | tf_op jit(solution)/shard_map/reduce_scatter | solution.py:70
  162.0 40.3 %reduce-scatter.6.cloned.1.call-done = bf16[16,128,192]{1,2,0:T(8,128)(2,1)} async-done(((bf16[16,128,768]{1,2,0:T(8,128)(2,1)}), bf16[16,128,192]{1,2,0:T(8,128)(2,1)}) %reduce-scatter.6.cloned.1.call-update) | async-done | bytes 786448 | tf_op jit(solution)/shard_map/reduce_scatter | solution.py:73
  202.4 10.7 %convolution_convert_fusion = bf16[16,128,2048]{2,1,0:T(8,128)(2,1)} fusion(bf16[16,192,2048]{2,1,0:T(8,128)(2,1)} %param.8, bf16[16,128,192]{1,2,0:T(8,128)(2,1)} %reduce-scatter.6.cloned.1.call-done, bf16[16,128,192]{1,2,0:T(8,128)(2,1)} %reduce-scatter.4.cloned.1.call-done), kind=kOutput, calls=%fused_computation.9 | convolution fusion | flops 1617952768 | bytes 22544384 | tf_op jit(solution)/shard_map/erf,efd->erd/dot_general | solution.py:78
  213.1 71.4 %reduce-scatter.8.cloned.1.call-done = bf16[16,128,512]{2,1,0:T(8,128)(2,1)} async-done(((bf16[16,128,2048]{2,1,0:T(8,128)(2,1)}), bf16[16,128,512]{2,1,0:T(8,128)(2,1)}) %reduce-scatter.8.cloned.1.call-update) | async-done | bytes 2097168 | tf_op jit(solution)/shard_map/reduce_scatter | solution.py:81
  284.5 3.2 copy.46
  287.6 5.6 %all-to-all-start = ((bf16[16,8,16,512]{3,2,0,1:T(8,128)(2,1)}), bf16[16,8,16,512]{3,2,0,1:T(8,128)(2,1)}, u32[]{:S(2)}, u32[]{:S(2)}) async-start(bf16[16,8,16,512]{3,2,0,1:T(8,128)(2,1)} %copy.46), calls=%async_computation.3 | async-start | bytes 4194304 | tf_op jit(solution)/shard_map/all_to_all | solution.py:85
  293.8 0.2 fusion.24
  294.4 11.1 %psum.7 = bf16[128,128]{1,0:T(8,128)(2,1)S(1)} all-reduce(bf16[128,128]{1,0:T(8,128)(2,1)S(1)} %convolution_convert_fusion.1), channel_id=1, replica_groups=mesh['narrow'=4,'wide'=8] {'narrow'}, use_global_device_ids=true, to_apply=%region_0.0 | all-reduce | flops 16384 | bytes 65536 | tf_op jit(solution)/shard_map/psum | solution.py:18
  305.5 0.4 select_reduce_fusion
  306.0 0.4 fusion.21
  306.5 35.0 %all-to-all-done = bf16[16,8,16,512]{3,2,0,1:T(8,128)(2,1)} async-done(((bf16[16,8,16,512]{3,2,0,1:T(8,128)(2,1)}), bf16[16,8,16,512]{3,2,0,1:T(8,128)(2,1)}, u32[]{:S(2)}, u32[]{:S(2)}) %all-to-all-start) | async-done | bytes 2097184 | tf_op jit(solution)/shard_map/all_to_all | solution.py:85
  341.5 1.8 copy.47
  343.2 4.0 %gather_fusion.1 = bf16[1024,512]{1,0:T(8,128)(2,1)S(1)} fusion(bf16[2048,512]{1,0:T(8,128)(2,1)S(1)} %bitcast.59, s32[1024]{0:T(1024)S(1)} %broadcast_clamp_fusion), kind=kCustom, calls=%fused_computation.1 | custom fusion | bytes 2101248 | tf_op jit(solution)/shard_map/gather | solution.py:87
  347.2 1.4 fusion.12
  (48 shorter events, 2.3 us)
Async XLA Ops:
  6.5 287.7 %copy-start = (bf16[512,128]{1,0:T(8,128)(2,1)S(1)}, bf16[512,128]{1,0:T(8,128)(2,1)}, u32[]{:S(2)}) copy-start(bf16[512,128]{1,0:T(8,128)(2,1)} %param.6) | copy-start | bytes 393220
  6.5 99.3 %all-gather.2.cloned.1.call-start = ((), (), s32[]{:S(2)}) async-start(), calls=%async_computation.4 | async-start | bytes 1179648 | tf_op jit(solution)/shard_map/all_gather | solution.py:38
  7.3 154.8 %reduce-scatter.4.cloned.1.call-start = ((), (), s32[]{:S(2)}) async-start(), calls=%async_computation.5 | async-start | bytes 3932160 | tf_op jit(solution)/shard_map/reduce_scatter | solution.py:70
  124.7 77.7 %reduce-scatter.6.cloned.1.call-start = ((), (), s32[]{:S(2)}) async-start(), calls=%async_computation.6 | async-start | bytes 3932160 | tf_op jit(solution)/shard_map/reduce_scatter | solution.py:73
  134.9 149.6 %reduce-scatter.8.cloned.1.call-start = ((), (), s32[]{:S(2)}) async-start(), calls=%async_computation.7 | async-start | bytes 10485760 | tf_op jit(solution)/shard_map/reduce_scatter | solution.py:81
  287.6 5.6 %copy-start.2 = (s32[128,8]{0,1:T(8,128)S(1)}, s32[128,8]{0,1:T(8,128)}, u32[]{:S(2)}) copy-start(s32[128,8]{0,1:T(8,128)} %param.9) | copy-start | bytes 12292
  287.6 53.8 %all-to-all-start = ((bf16[16,8,16,512]{3,2,0,1:T(8,128)(2,1)}), bf16[16,8,16,512]{3,2,0,1:T(8,128)(2,1)}, u32[]{:S(2)}, u32[]{:S(2)}) async-start(bf16[16,8,16,512]{3,2,0,1:T(8,128)(2,1)} %copy.46), calls=%async_computation.3 | async-start | bytes 4194304 | tf_op jit(solution)/shard_map/all_to_all | solution.py:85
  293.3 0.9 copy-start.1
Sparse Core Ops, SparseCore 0:
  9.5 42.9 all-gather.1
  124.8 37.1 reduce-scatter.3
  164.6 37.7 reduce-scatter.5
  213.2 71.2 reduce-scatter.7
where the time goes:
time: 356 us; the launch traced here: 355 us
  waiting for transfers between devices  175 us (49%)
  local copies, waits for them, and re-layouts  51.5 us (14%)
  other arithmetic  40 us (11%)
  blocking collectives  39 us (11%)
  matrix products  30.7 us (9%)
  between operations  13.4 us (4%)
  starting transfers between devices  5.94 us (2%)
    reduce_scatter x1, waiting for transfers between devices, local(): lax.psum_scatter(expert_terms.astype(jnp.bfloat16), 'narrow', scatter_dim...  71.4 us
    reduce_scatter x1, waiting for transfers between devices, local(): lax.psum_scatter(up_terms.astype(jnp.bfloat16), 'narrow', scatter_dimensi...  40.3 us
    another operation x6, other arithmetic  36.5 us
    all_to_all x1, waiting for transfers between devices, local(): lax.all_to_all(expert_out, 'wide', split_axis=1, concat_axis=1, tiled=True)  35 us
    scatter x1, local copies, waits for them, and re-layouts, local(): slot_table = jnp.full((slot_total,), blocks * tok_count, jnp.int32).at[de...  30.4 us
    all_gather x1, blocking collectives, local(): lax.all_gather(expert_ids.astype(jnp.bfloat16), 'wide', axis=0, tiled=True)  27.9 us
    reduce_scatter x1, waiting for transfers between devices, local(): lax.psum_scatter(gate_terms.astype(jnp.bfloat16), 'narrow', scatter_dimen...  27.1 us
    psum x1, blocking collectives, local(): lax.psum(jnp.dot(normed, router_weight, preferred_element_type=jnp.float3...  11.1 us
  transfers between devices with their start and end apart: 5, of which 4 were waited for; matrix products, arithmetic and copies ran while one was open for 23% of the time, Pallas kernels for 0%

commit v1 on v0

--- a/solution.py
+++ b/solution.py
@@ -5,6 +5,22 @@
 
 TOPK = 8
 CAP = 16
+
+
+def exchange_in_pairs(value, axis, split, join):
+    ways, here = (lax.axis_size(axis), lax.axis_index(axis))
+    width = value.shape[split] // ways
+    lengths = list(value.shape)
+    lengths[split] = width
+    height = lengths[join]
+    lengths[join] = height * ways
+    full = jnp.zeros(lengths, value.dtype)
+    for mask in range(ways):
+        part = lax.dynamic_slice_in_dim(value, (here ^ mask) * width, width, axis=split)
+        if mask:
+            part = lax.ppermute(part, axis, [(d, d ^ mask) for d in range(ways)])
+        full = lax.dynamic_update_slice_in_dim(full, part, (here ^ mask) * height, axis=join)
+    return full
 
 
 def local(normed, router_weight, gate_up_weight, down_weight, expert_ids):
@@ -82,7 +98,7 @@
         expert_terms.astype(jnp.bfloat16), "narrow", scatter_dimension=2, tiled=True
     )
     expert_out = expert_out.reshape(local_experts, blocks, capacity, share_width)
-    returned = lax.all_to_all(expert_out, "wide", split_axis=1, concat_axis=1, tiled=True)
+    returned = exchange_in_pairs(expert_out, "wide", 1, 1)
     flat_out = returned.reshape(slot_total, share_width)
     picked = flat_out[out_index].reshape(tok_count, TOPK, share_width)
     combined = jnp.sum(weights[:, :, None] * picked.astype(jnp.float32), axis=1)

time: 356 us -> 349 us (0.980)
  the two profiles are of different devices: /device:TPU:0 before, /device:TPU:16 now
where the time goes in v1:
time: 349 us; the launch traced here: 348 us
  waiting for transfers between devices  172 us (49%)
  local copies, waits for them, and re-layouts  49.1 us (14%)
  other arithmetic  39.9 us (11%)
  blocking collectives  34.2 us (10%)
  matrix products  30.7 us (9%)
  between operations  13.6 us (4%)
  starting transfers between devices  8.51 us (2%)
    reduce_scatter x1, waiting for transfers between devices, local(): lax.psum_scatter(expert_terms.astype(jnp.bfloat16), 'narrow', scatter_dim...  58.2 us
    ppermute x7, waiting for transfers between devices, exchange_in_pairs(): part = lax.ppermute(part, axis, [(d, d ^ mask) for d in range(ways)])  43.5 us
    reduce_scatter x1, waiting for transfers between devices, local(): lax.psum_scatter(up_terms.astype(jnp.bfloat16), 'narrow', scatter_dimensi...  40.3 us
    another operation x6, other arithmetic  36.5 us
    scatter x1, local copies, waits for them, and re-layouts, local(): slot_table = jnp.full((slot_total,), blocks * tok_count, jnp.int32).at[de...  30.4 us
    reduce_scatter x1, waiting for transfers between devices, local(): lax.psum_scatter(gate_terms.astype(jnp.bfloat16), 'narrow', scatter_dimen...  29.5 us
    all_gather x1, blocking collectives, local(): lax.all_gather(expert_ids.astype(jnp.bfloat16), 'wide', axis=0, tiled=True)  23.8 us
    dot_general x1, matrix products, local(): jnp.einsum('erf,efd->erd', hidden, down_weight, preferred_element_type=jn...  10.7 us
  transfers between devices with their start and end apart: 11, of which 9 were waited for; matrix products, arithmetic and copies ran while one was open for 24% of the time, Pallas kernels for 0%

profile of v1, /device:TPU:16, one launch (start us, length us, event | category | flops | bytes accessed | tf_op | source)
XLA Modules:
  0.0 348.4 jit_solution(1657535062200965172)
XLA Ops:
  6.5 0.7 all-gather.2.cloned.1.call-update
  7.3 0.7 convert_element_type.56
  8.0 23.8 %all_gather.7 = bf16[1024,8]{0,1:T(8,128)(2,1)S(1)} all-gather(bf16[128,8]{0,1:T(8,128)(2,1)S(1)} %convert_element_type.56), channel_id=1, replica_groups=mesh['narrow'=4,'wide'=8] {'wide'}, dimensions={0}, use_global_device_ids=true | all-gather | bytes 18432 | tf_op jit(solution)/shard_map/all_gather | solution.py:55
  32.7 36.0 %reduce-window.14 = s32[8,16,8,128]{3,2,1,0:T(8,128)S(1)} reduce-window(s32[8,16,8,128]{3,2,1,0:T(8,128)S(1)} %fusion.26, s32[]{:T(128)} %constant.35.clone.1), window={size=1x1x1x128 pad=0_0x0_0x0_0x127_0}, to_apply=%region_3.0 | reduce-window | flops 16646144 | bytes 1048580 | tf_op jit(solution)/shard_map/reduce-window
  68.9 0.5 copy.26
  71.3 30.4 %scatter_custom_fusion = s32[2048]{0:T(1024)S(1)} fusion(s32[8192]{0:T(1024)S(1)} %bitcast.67, s32[8192]{0:T(1024)S(1)} %bitcast.68, s32[]{:T(128)} %constant.29.clone.1), kind=kCustom, calls=%fused_computation.79 | custom fusion | bytes 8196 | tf_op jit(solution)/shard_map/scatter | solution.py:74
  101.8 1.3 concatenate.3
  103.1 7.5 %gather_fusion = bf16[2048,512]{1,0:T(8,128)(2,1)S(1)} fusion(bf16[1025,512]{1,0:T(8,128)(2,1)S(1)} %concatenate.3, s32[2048]{0:T(1024)S(1)} %fusion.28), kind=kCustom, calls=%fused_computation | custom fusion | bytes 4202496 | tf_op jit(solution)/shard_map/gather | solution.py:77
  110.6 9.9 %fusion.6 = bf16[16,128,768]{1,2,0:T(8,128)(2,1)} fusion(bf16[16,128,512]{2,1,0:T(8,128)(2,1)S(1)} %bitcast.60, bf16[16,2,512,768]{3,2,1,0:T(8,128)(2,1)} %param.7), kind=kOutput, calls=%fused_computation.10 | convolution fusion | flops 1612185600 | bytes 17825792 | tf_op jit(solution)/shard_map/erd,edf->erf/dot_general | solution.py:79
  120.8 10.0 %fusion.9 = bf16[16,128,768]{1,2,0:T(8,128)(2,1)} fusion(bf16[16,128,512]{2,1,0:T(8,128)(2,1)S(1)} %bitcast.61, bf16[16,2,512,768]{3,2,1,0:T(8,128)(2,1)} %param.7), kind=kOutput, calls=%fused_computation.11 | convolution fusion | flops 1612185600 | bytes 17825792 | tf_op jit(solution)/shard_map/erd,edf->erf/dot_general | solution.py:82
  130.8 29.5 %reduce-scatter.4.cloned.1.call-done = bf16[16,128,192]{1,2,0:T(8,128)(2,1)} async-done(((bf16[16,128,768]{1,2,0:T(8,128)(2,1)}), bf16[16,128,192]{1,2,0:T(8,128)(2,1)}) %reduce-scatter.4.cloned.1.call-update) | async-done | bytes 786448 | tf_op jit(solution)/shard_map/reduce_scatter | solution.py:86
  160.4 40.3 %reduce-scatter.6.cloned.1.call-done = bf16[16,128,192]{1,2,0:T(8,128)(2,1)} async-done(((bf16[16,128,768]{1,2,0:T(8,128)(2,1)}), bf16[16,128,192]{1,2,0:T(8,128)(2,1)}) %reduce-scatter.6.cloned.1.call-update) | async-done | bytes 786448 | tf_op jit(solution)/shard_map/reduce_scatter | solution.py:89
  200.7 10.7 %convolution_convert_fusion = bf16[16,128,2048]{2,1,0:T(8,128)(2,1)} fusion(bf16[16,192,2048]{2,1,0:T(8,128)(2,1)} %param.8, bf16[16,128,192]{1,2,0:T(8,128)(2,1)} %reduce-scatter.6.cloned.1.call-done, bf16[16,128,192]{1,2,0:T(8,128)(2,1)} %reduce-scatter.4.cloned.1.call-done), kind=kOutput, calls=%fused_computation.9 | convolution fusion | flops 1617952768 | bytes 22544384 | tf_op jit(solution)/shard_map/erf,efd->erd/dot_general | solution.py:94
  211.5 0.6 copy-done.3
  213.2 10.4 %psum.7 = bf16[128,128]{1,0:T(8,128)(2,1)S(1)} all-reduce(bf16[128,128]{1,0:T(8,128)(2,1)S(1)} %convolution_convert_fusion.1), channel_id=1, replica_groups=mesh['narrow'=4,'wide'=8] {'narrow'}, use_global_device_ids=true, to_apply=%region_0.0 | all-reduce | flops 16384 | bytes 65536 | tf_op jit(solution)/shard_map/psum | solution.py:34
  224.1 0.4 fusion.21
  224.6 58.2 %reduce-scatter.8.cloned.1.call-done = bf16[16,128,512]{2,1,0:T(8,128)(2,1)} async-done(((bf16[16,128,2048]{2,1,0:T(8,128)(2,1)}), bf16[16,128,512]{2,1,0:T(8,128)(2,1)}) %reduce-scatter.8.cloned.1.call-update) | async-done | bytes 2097168 | tf_op jit(solution)/shard_map/reduce_scatter | solution.py:97
  283.1 1.3 copy-done.1
  284.7 1.5 collective-permute-start
  286.2 1.5 collective-permute-start.1
  287.8 0.6 collective-permute-start.2
  288.3 0.5 collective-permute-start.3
  288.8 3.3 collective-permute-start.4
  292.2 0.7 collective-permute-done
  292.9 0.5 collective-permute-start.5
  293.5 9.9 %collective-permute-done.1 = bf16[16,1,16,512]{3,2,1,0:T(8,128)(2,1)S(1)} collective-permute-done((bf16[16,1,16,512]{3,2,1,0:T(8,128)(2,1)S(1)}, bf16[16,1,16,512]{3,2,1,0:T(8,128)(2,1)S(1)}, u32[]{:S(2)}, u32[]{:S(2)}) %collective-permute-start.1) | collective-permute-done | bytes 262176 | tf_op jit(solution)/shard_map/ppermute | solution.py:21
  303.6 3.8 %collective-permute-done.2 = bf16[16,1,16,512]{3,2,1,0:T(8,128)(2,1)S(1)} collective-permute-done((bf16[16,1,16,512]{3,2,1,0:T(8,128)(2,1)S(1)}, bf16[16,1,16,512]{3,2,1,0:T(8,128)(2,1)S(1)}, u32[]{:S(2)}, u32[]{:S(2)}) %collective-permute-start.2) | collective-permute-done | bytes 262176 | tf_op jit(solution)/shard_map/ppermute | solution.py:21
  307.5 16.2 %collective-permute-done.4 = bf16[16,1,16,512]{3,2,1,0:T(8,128)(2,1)S(1)} collective-permute-done((bf16[16,1,16,512]{3,2,1,0:T(8,128)(2,1)S(1)}, bf16[16,1,16,512]{3,2,1,0:T(8,128)(2,1)S(1)}, u32[]{:S(2)}, u32[]{:S(2)}) %collective-permute-start.4) | collective-permute-done | bytes 262176 | tf_op jit(solution)/shard_map/ppermute | solution.py:21
  323.6 8.5 %collective-permute-done.5 = bf16[16,1,16,512]{3,2,1,0:T(8,128)(2,1)S(1)} collective-permute-done((bf16[16,1,16,512]{3,2,1,0:T(8,128)(2,1)S(1)}, bf16[16,1,16,512]{3,2,1,0:T(8,128)(2,1)S(1)}, u32[]{:S(2)}, u32[]{:S(2)}) %collective-permute-start.5) | collective-permute-done | bytes 262176 | tf_op jit(solution)/shard_map/ppermute | solution.py:21
  332.2 4.4 %collective-permute-done.6 = bf16[16,1,16,512]{3,2,1,0:T(8,128)(2,1)S(1)} collective-permute-done((bf16[16,1,16,512]{3,2,1,0:T(8,128)(2,1)S(1)}, bf16[16,1,16,512]{3,2,1,0:T(8,128)(2,1)S(1)}, u32[]{:S(2)}, u32[]{:S(2)}) %collective-permute-start.6) | collective-permute-done | bytes 262176 | tf_op jit(solution)/shard_map/ppermute | solution.py:21
  336.6 4.0 %gather_fusion.1 = bf16[1024,512]{1,0:T(8,128)(2,1)S(1)} fusion(bf16[2048,512]{1,0:T(8,128)(2,1)S(1)} %bitcast.59, s32[1024]{0:T(1024)S(1)} %broadcast_clamp_fusion), kind=kCustom, calls=%fused_computation.1 | custom fusion | bytes 2101248 | tf_op jit(solution)/shard_map/gather | solution.py:103
  340.6 1.3 fusion.12
  (69 shorter events, 5.7 us)
Async XLA Ops:
  6.5 206.5 %copy-start = (bf16[512,128]{1,0:T(8,128)(2,1)S(1)}, bf16[512,128]{1,0:T(8,128)(2,1)}, u32[]{:S(2)}) copy-start(bf16[512,128]{1,0:T(8,128)(2,1)} %param.6) | copy-start | bytes 393220
  6.5 95.2 %all-gather.2.cloned.1.call-start = ((), (), s32[]{:S(2)}) async-start(), calls=%async_computation.3 | async-start | bytes 1179648 | tf_op jit(solution)/shard_map/all_gather | solution.py:54
  7.3 153.1 %reduce-scatter.4.cloned.1.call-start = ((), (), s32[]{:S(2)}) async-start(), calls=%async_computation.4 | async-start | bytes 3932160 | tf_op jit(solution)/shard_map/reduce_scatter | solution.py:86
  120.6 80.2 %reduce-scatter.6.cloned.1.call-start = ((), (), s32[]{:S(2)}) async-start(), calls=%async_computation.5 | async-start | bytes 3932160 | tf_op jit(solution)/shard_map/reduce_scatter | solution.py:89
  130.8 152.1 %reduce-scatter.8.cloned.1.call-start = ((), (), s32[]{:S(2)}) async-start(), calls=%async_computation.6 | async-start | bytes 10485760 | tf_op jit(solution)/shard_map/reduce_scatter | solution.py:97
  211.4 0.7 copy-start.3
  211.4 1.6 copy-start.2
  282.8 1.6 copy-start.1
  284.7 8.2 %collective-permute-start = (bf16[16,1,16,512]{3,2,1,0:T(8,128)(2,1)S(1)}, bf16[16,1,16,512]{3,2,1,0:T(8,128)(2,1)S(1)}, u32[]{:S(2)}, u32[]{:S(2)}) collective-permute-start(bf16[16,1,16,512]{3,2,1,0:T(8,128)(2,1)S(1)} %get-tuple-element.11), channel_id=1, source_target_pairs={{0,1},{1,0},{2,3},{3,2},{4,5},{5,4},{6,7},{7,6},{8,9},{9,8},{10,11... | collective-permute-start | bytes 786440 | tf_op jit(solution)/shard_map/ppermute | solution.py:21
  286.2 17.1 %collective-permute-start.1 = (bf16[16,1,16,512]{3,2,1,0:T(8,128)(2,1)S(1)}, bf16[16,1,16,512]{3,2,1,0:T(8,128)(2,1)S(1)}, u32[]{:S(2)}, u32[]{:S(2)}) collective-permute-start(bf16[16,1,16,512]{3,2,1,0:T(8,128)(2,1)S(1)} %get-tuple-element.10), channel_id=1, source_target_pairs={{0,2},{1,3},{2,0},{3,1},{4,6},{5,7},{6,4},{7,5},{8,10},{9,11},{10,... | collective-permute-start | bytes 786440 | tf_op jit(solution)/shard_map/ppermute | solution.py:21
  287.8 19.6 %collective-permute-start.2 = (bf16[16,1,16,512]{3,2,1,0:T(8,128)(2,1)S(1)}, bf16[16,1,16,512]{3,2,1,0:T(8,128)(2,1)S(1)}, u32[]{:S(2)}, u32[]{:S(2)}) collective-permute-start(bf16[16,1,16,512]{3,2,1,0:T(8,128)(2,1)S(1)} %get-tuple-element.9), channel_id=1, source_target_pairs={{0,3},{1,2},{2,1},{3,0},{4,7},{5,6},{6,5},{7,4},{8,11},{9,10},{10,... | collective-permute-start | bytes 786440 | tf_op jit(solution)/shard_map/ppermute | solution.py:21
  288.3 19.1 %collective-permute-start.3 = (bf16[16,1,16,512]{3,2,1,0:T(8,128)(2,1)S(1)}, bf16[16,1,16,512]{3,2,1,0:T(8,128)(2,1)S(1)}, u32[]{:S(2)}, u32[]{:S(2)}) collective-permute-start(bf16[16,1,16,512]{3,2,1,0:T(8,128)(2,1)S(1)} %get-tuple-element.8), channel_id=1, source_target_pairs={{0,4},{1,5},{2,6},{3,7},{4,0},{5,1},{6,2},{7,3},{8,12},{9,13},{10,... | collective-permute-start | bytes 786440 | tf_op jit(solution)/shard_map/ppermute | solution.py:21
  288.8 34.8 %collective-permute-start.4 = (bf16[16,1,16,512]{3,2,1,0:T(8,128)(2,1)S(1)}, bf16[16,1,16,512]{3,2,1,0:T(8,128)(2,1)S(1)}, u32[]{:S(2)}, u32[]{:S(2)}) collective-permute-start(bf16[16,1,16,512]{3,2,1,0:T(8,128)(2,1)S(1)} %get-tuple-element.7), channel_id=1, source_target_pairs={{0,5},{1,4},{2,7},{3,6},{4,1},{5,0},{6,3},{7,2},{8,13},{9,12},{10,... | collective-permute-start | bytes 786440 | tf_op jit(solution)/shard_map/ppermute | solution.py:21
  292.9 39.2 %collective-permute-start.5 = (bf16[16,1,16,512]{3,2,1,0:T(8,128)(2,1)S(1)}, bf16[16,1,16,512]{3,2,1,0:T(8,128)(2,1)S(1)}, u32[]{:S(2)}, u32[]{:S(2)}) collective-permute-start(bf16[16,1,16,512]{3,2,1,0:T(8,128)(2,1)S(1)} %get-tuple-element.6), channel_id=1, source_target_pairs={{0,6},{1,7},{2,4},{3,5},{4,2},{5,3},{6,0},{7,1},{8,14},{9,15},{10,... | collective-permute-start | bytes 786440 | tf_op jit(solution)/shard_map/ppermute | solution.py:21
  303.3 33.2 %collective-permute-start.6 = (bf16[16,1,16,512]{3,2,1,0:T(8,128)(2,1)S(1)}, bf16[16,1,16,512]{3,2,1,0:T(8,128)(2,1)S(1)}, u32[]{:S(2)}, u32[]{:S(2)}) collective-permute-start(bf16[16,1,16,512]{3,2,1,0:T(8,128)(2,1)S(1)} %get-tuple-element.5), channel_id=1, source_target_pairs={{0,7},{1,6},{2,5},{3,4},{4,3},{5,2},{6,1},{7,0},{8,15},{9,14},{10,... | collective-permute-start | bytes 786440 | tf_op jit(solution)/shard_map/ppermute | solution.py:21
Sparse Core Ops, SparseCore 0:
  9.5 39.5 all-gather.1
  120.7 39.6 reduce-scatter.3
  162.9 37.7 reduce-scatter.5
  211.6 71.2 reduce-scatter.7
